TPU v7x, 256 devices: a whole 4x4x8 slice. The times are simulated.
256 devices in a mesh: leaf: 16 (over z, core), list: 16 (over y, x).
Axes of the slice: x: 4, y: 4, z: 8, core: 2. Of those that a mesh axis runs over, the one named last changes fastest.
Arguments:
- panel_charges: bfloat16 [4096, 64, 256], P(('leaf', 'list')), may hold values from -6 to 6
- leaf_basis: bfloat16 [4096, 64, 256], P(('leaf', 'list')), may hold values from -0.375 to 0.375
- near_blocks: bfloat16 [4096, 4, 256, 256], P(('leaf', 'list')), may hold values from -0.1875 to 0.1875
- near_list: int32 [4096, 4], P(('leaf', 'list')), may hold values from 0 to 15, as said below
- far_list: int32 [4096, 8], P(('leaf', 'list')), may hold values from 0 to 255, as said below
- far_count: int32 [4096], P(('leaf', 'list')), may hold values from 1 to 8, as said below
- far_coupling: bfloat16 [4096, 8, 64, 64], P(('leaf', 'list')), may hold values from -0.25 to 0.25
- leaf_transfer: float32 [4096, 64, 64], P(('leaf', 'list')), may hold values from -0.4375 to 0.4375
- device_transfer: float32 [16, 16, 64, 64], P('leaf', 'list'), may hold values from -0.375 to 0.375
- tree_transfer: float32 [24, 64, 64], replicated, may hold values from -0.75 to 0.75
- level_coupling: float32 [28, 4, 64, 64], replicated, may hold values from -0.4375 to 0.4375
Outputs:
- potential: bfloat16 [4096, 64, 256], P(('leaf', 'list'))
Inputs may be any that keep to these rules, and one draw needn't show every extreme that they name: `far_list`: each row names 8 different leaves of the leaf's group subtree, none on the leaf's own device; the 16 leaves of one device name, over all their slots, exactly 8 different leaves of each other device of the group. Slots at and after far_count[c] are unused. `near_list`: each row names 4 different leaves of the leaf's own device, the first being the leaf itself.
All inputs are finite; a program needn't handle non-finite values.
Results may differ from a plain program's by a relative error of at most 0.0053.
Values may be sent and summed in bfloat16 or wider, within the bound.
A program may use at most 64 MiB of HBM per device.

v0:
```python
import jax
import jax.numpy as jnp
from jax import lax
from jax.sharding import PartitionSpec as P

highest = lax.Precision.HIGHEST
offsets = (-3, -2, 2, 3)


def partner(array, axis, distance):
    return lax.ppermute(array, axis, [(i, i ^ 1 << distance) for i in range(lax.axis_size(axis))])


def shifted(array, axis, by):
    length = lax.axis_size(axis)
    pairs = [(i, i + by) for i in range(length) if 0 <= i + by < length]
    return lax.ppermute(array, axis, pairs)


def pick_usable(offset, parity):
    if offset == 3:
        return parity == 0
    if offset == -3:
        return parity == 1
    return parity >= 0


def upper_exchange(group_node, tree_transfer, level_coupling):
    leaf_count = lax.axis_size("leaf")
    depth = leaf_count.bit_length() - 2
    position = lax.axis_index("leaf")
    nodes = [group_node]
    for height in range(depth - 1):
        begin_row = 2 * leaf_count - 2 * (leaf_count >> height)
        matrix = tree_transfer[begin_row + (position >> height)]
        own_part = jnp.dot(nodes[-1], matrix, precision=highest)
        nodes.append(own_part + partner(own_part, "leaf", height))
    coupled = []
    for height in range(depth):
        begin_row = 2 * leaf_count - 2 * (leaf_count >> height)
        matrices = level_coupling[begin_row + (position >> height)]
        parity = (position >> height) % 2
        summed = jnp.zeros_like(group_node)
        for slot_index, offset in enumerate(offsets):
            source = shifted(nodes[height], "leaf", -offset * (1 << height))
            contribution = jnp.dot(source, matrices[slot_index].T, precision=highest)
            summed = summed + jnp.where(
                pick_usable(offset, parity), contribution, jnp.zeros((), jnp.float32)
            )
        coupled.append(summed)
    result = coupled[-1]
    for height in reversed(range(depth - 1)):
        begin_row = 2 * leaf_count - 2 * (leaf_count >> height)
        matrix = tree_transfer[begin_row + (position >> height)]
        result = coupled[height] + jnp.dot(result, matrix.T, precision=highest)
    return result


def on_device(
    panel_charges,
    leaf_basis,
    near_blocks,
    near_list,
    far_list,
    far_count,
    far_coupling,
    leaf_transfer,
    device_transfer,
    tree_transfer,
    level_coupling,
):
    leaf_local = panel_charges.shape[0]
    far_slots = far_list.shape[1]
    near_slots = near_list.shape[1]
    skeleton = jnp.einsum(
        "crm,ckm->crk", panel_charges, leaf_basis, preferred_element_type=jnp.float32
    ).astype(jnp.bfloat16)
    device_node = jnp.einsum(
        "irb,iba->ra", skeleton.astype(jnp.float32), leaf_transfer, precision=highest
    )
    device_term = jnp.dot(device_node, device_transfer[0, 0], precision=highest)
    group_node = lax.psum(device_term, "list")
    top_down = upper_exchange(group_node, tree_transfer, level_coupling)
    device_down = jnp.dot(top_down, device_transfer[0, 0].T, precision=highest)
    from_above = jnp.einsum("rd,ild->irl", device_down, leaf_transfer, precision=highest)
    row_width = skeleton.shape[1] * skeleton.shape[2]
    flattened = skeleton.reshape(leaf_local, row_width)
    wanted = far_list.reshape(-1)
    usable = (jnp.arange(far_slots, dtype=jnp.int32)[None, :] < far_count[:, None]).reshape(-1)
    piece = lax.all_gather(flattened, "list", axis=0, tiled=True)
    columns = jnp.arange(piece.shape[0], dtype=jnp.int32)
    hits = ((wanted[:, None] == columns[None, :]) & usable[:, None]).astype(jnp.bfloat16)
    collected = jnp.dot(hits, piece, preferred_element_type=jnp.float32)
    selected = collected.astype(jnp.bfloat16)
    selected = selected.reshape(leaf_local, far_slots, skeleton.shape[1], skeleton.shape[2])
    leaf_coupled = jnp.einsum(
        "ckrb,ckab->cra", selected, far_coupling, preferred_element_type=jnp.float32
    )
    coefficients = (leaf_coupled + from_above).astype(jnp.bfloat16)
    far_field = jnp.einsum(
        "crk,ckm->crm", coefficients, leaf_basis, preferred_element_type=jnp.float32
    )
    neighbours = jnp.take(panel_charges, near_list.reshape(-1), axis=0)
    neighbours = neighbours.reshape(
        leaf_local, near_slots, panel_charges.shape[1], panel_charges.shape[2]
    )
    near_field = jnp.einsum(
        "ckrm,cknm->crn", neighbours, near_blocks, preferred_element_type=jnp.float32
    )
    return (far_field + near_field).astype(jnp.bfloat16)


def solution(mesh):
    in_specs = (
        P(("leaf", "list"), None, None),
        P(("leaf", "list"), None, None),
        P(("leaf", "list"), None, None, None),
        P(("leaf", "list"), None),
        P(("leaf", "list"), None),
        P(("leaf", "list")),
        P(("leaf", "list"), None, None, None),
        P(("leaf", "list"), None, None),
        P("leaf", "list", None, None),
        P(),
        P(),
    )
    out_specs = P(("leaf", "list"), None, None)
    return jax.shard_map(
        on_device, mesh=mesh, in_specs=in_specs, out_specs=out_specs, check_vma=False
    )
```

profile of v0, /device:TPU:32, one launch (start us, length us, event | category | flops | bytes accessed | tf_op | source)
XLA Modules:
  0.0 177.3 jit_solution(7116425798900764517)
XLA Ops:
  6.5 1.6 convolution_convert_fusion.1
  8.2 1.4 convolution_bitcast_fusion.3
  10.5 74.6 %psum.7 = f32[64,64]{1,0:T(8,128)S(1)} all-reduce(f32[64,64]{1,0:T(8,128)S(1)} %fusion.34), channel_id=1, replica_groups=mesh['leaf'=16,'list'=16] {'list'}, use_global_device_ids=true, to_apply=%region_0.0 | all-reduce | flops 4096 | bytes 32768 | tf_op jit(solution)/shard_map/psum | solution.py:82
  85.1 1.3 collective-permute-start.3
  86.4 2.0 %collective-permute-start.2 = (f32[64,64]{1,0:T(8,128)S(1)}, f32[64,64]{1,0:T(8,128)S(1)}, u32[]{:S(2)}, u32[]{:S(2)}) collective-permute-start(f32[64,64]{1,0:T(8,128)S(1)} %psum.7), channel_id=1, source_target_pairs={{32,0},{48,16},{64,32},{80,48},{96,64},{112,80},{128,96},{144,112}... | collective-permute-start | bytes 49160 | tf_op jit(solution)/shard_map/ppermute | solution.py:17
  88.5 4.3 %collective-permute-start.1 = (f32[64,64]{1,0:T(8,128)S(1)}, f32[64,64]{1,0:T(8,128)S(1)}, u32[]{:S(2)}, u32[]{:S(2)}) collective-permute-start(f32[64,64]{1,0:T(8,128)S(1)} %psum.7), channel_id=1, source_target_pairs={{0,32},{16,48},{32,64},{48,80},{64,96},{80,112},{96,128},{112,144}... | collective-permute-start | bytes 49160 | tf_op jit(solution)/shard_map/ppermute | solution.py:17
  92.8 3.4 %collective-permute-start = (f32[64,64]{1,0:T(8,128)S(1)}, f32[64,64]{1,0:T(8,128)S(1)}, u32[]{:S(2)}, u32[]{:S(2)}) collective-permute-start(f32[64,64]{1,0:T(8,128)S(1)} %psum.7), channel_id=1, source_target_pairs={{0,48},{16,64},{32,80},{48,96},{64,112},{80,128},{96,144},{112,160... | collective-permute-start | bytes 49160 | tf_op jit(solution)/shard_map/ppermute | solution.py:17
  98.1 3.3 %collective-permute-start.4 = (f32[64,64]{1,0:T(8,128)S(1)}, f32[64,64]{1,0:T(8,128)S(1)}, u32[]{:S(2)}, u32[]{:S(2)}) collective-permute-start(f32[64,64]{1,0:T(8,128)S(1)} %fusion.31), channel_id=1, source_target_pairs={{0,16},{16,0},{32,48},{48,32},{64,80},{80,64},{96,112},{112,96},{1... | collective-permute-start | bytes 49160 | tf_op jit(solution)/shard_map/ppermute | solution.py:11
  103.1 2.0 %gather_fusion = bf16[64,64,256]{2,1,0:T(8,128)(2,1)} fusion(bf16[16,64,256]{2,1,0:T(8,128)(2,1)S(1)} %copy-done.1, s32[1024]{0:T(1024)S(1)} %pad_clamp_fusion), kind=kCustom, calls=%fused_computation | custom fusion | bytes 4194560 | tf_op jit(solution)/shard_map/jit(_take)/gather | solution.py:103
  105.1 6.8 %fusion.3 = f32[16,64,256]{2,1,0:T(8,128)S(1)} fusion(bf16[16,4,256,256]{3,2,1,0:T(8,128)(2,1)} %param.13, bf16[16,4,64,256]{3,2,1,0:T(8,128)(2,1)} %bitcast.100, pred[16,4]{1,0:T(8,128)(4,1)S(1)} %copy.16), kind=kOutput, calls=%fused_computation.5 | convolution fusion | flops 537919488 | bytes 11534400 | tf_op jit(solution)/shard_map/ckrm,cknm->crn/dot_general | solution.py:107
  112.3 1.3 collective-permute-start.8
  114.5 1.3 collective-permute-start.7
  116.8 5.5 %collective-permute-start.6 = (f32[64,64]{1,0:T(8,128)S(1)}, f32[64,64]{1,0:T(8,128)S(1)}, u32[]{:S(2)}, u32[]{:S(2)}) collective-permute-start(f32[64,64]{1,0:T(8,128)S(1)} %add.117), channel_id=1, source_target_pairs={{0,64},{16,80},{32,96},{48,112},{64,128},{80,144},{96,160},{112,17... | collective-permute-start | bytes 49160 | tf_op jit(solution)/shard_map/ppermute | solution.py:17
  124.7 2.6 %collective-permute-done.9 = f32[64,64]{1,0:T(8,128)S(1)} collective-permute-done((f32[64,64]{1,0:T(8,128)S(1)}, f32[64,64]{1,0:T(8,128)S(1)}, u32[]{:S(2)}, u32[]{:S(2)}) %collective-permute-start.9) | collective-permute-done | bytes 16416 | tf_op jit(solution)/shard_map/ppermute | solution.py:11
  127.3 7.4 %collective-permute-start.5 = (f32[64,64]{1,0:T(8,128)S(1)}, f32[64,64]{1,0:T(8,128)S(1)}, u32[]{:S(2)}, u32[]{:S(2)}) collective-permute-start(f32[64,64]{1,0:T(8,128)S(1)} %add.117), channel_id=1, source_target_pairs={{0,96},{16,112},{32,128},{48,144},{64,160},{80,176},{96,192},{112,... | collective-permute-start | bytes 49160 | tf_op jit(solution)/shard_map/ppermute | solution.py:17
  134.8 1.3 collective-permute-start.13
  137.1 1.3 collective-permute-start.12
  139.3 8.5 %collective-permute-start.11 = (f32[64,64]{1,0:T(8,128)S(1)}, f32[64,64]{1,0:T(8,128)S(1)}, u32[]{:S(2)}, u32[]{:S(2)}) collective-permute-start(f32[64,64]{1,0:T(8,128)S(1)} %add.125), channel_id=1, source_target_pairs={{0,128},{16,144},{32,160},{48,176},{64,192},{80,208},{96,224},{112... | collective-permute-start | bytes 49160 | tf_op jit(solution)/shard_map/ppermute | solution.py:17
  148.8 1.3 collective-permute-start.10
  158.0 3.1 %convolution_convert_fusion = bf16[128,4096]{1,0:T(8,128)(2,1)} fusion(bf16[256,4096]{1,0:T(8,128)(2,1)} %all-gather.2.cloned.1.call-done, s32[128]{0:T(128)S(1)} %eq.37, pred[128]{0:T(512)(128)(4,1)S(1)} %lt.70), kind=kOutput, calls=%fused_computation.1 | convolution fusion | flops 269025280 | bytes 3146368 | tf_op jit(solution)/shard_map/dot_general | solution.py:93
  161.1 4.3 %reshape.87 = bf16[16,8,64,64]{3,2,1,0:T(8,128)(2,1)} reshape(bf16[128,4096]{1,0:T(8,128)(2,1)} %convolution_convert_fusion) | data formatting | bytes 2097152 | tf_op jit(solution)/shard_map/reshape | solution.py:95
  165.3 2.4 %convolution_bitcast_fusion = f32[16,64,64]{2,1,0:T(8,128)S(1)} fusion(bf16[16,8,64,64]{3,2,1,0:T(8,128)(2,1)} %reshape.87, bf16[16,8,64,64]{3,2,1,0:T(8,128)(2,1)S(1)} %copy-done), kind=kOutput, calls=%fused_computation.8 | convolution fusion | flops 67108864 | bytes 2359296 | tf_op jit(solution)/shard_map/ckrb,ckab->cra/dot_general | solution.py:96
  167.7 1.6 fusion.8
  169.3 1.1 fusion.6
  (62 shorter events, 19.7 us)
Async XLA Ops:
  6.5 158.8 %copy-start = (bf16[16,8,64,64]{3,2,1,0:T(8,128)(2,1)S(1)}, bf16[16,8,64,64]{3,2,1,0:T(8,128)(2,1)}, u32[]{:S(2)}) copy-start(bf16[16,8,64,64]{3,2,1,0:T(8,128)(2,1)} %param.17) | copy-start | bytes 3145732
  6.5 96.5 %copy-start.1 = (bf16[16,64,256]{2,1,0:T(8,128)(2,1)S(1)}, bf16[16,64,256]{2,1,0:T(8,128)(2,1)}, u32[]{:S(2)}) copy-start(bf16[16,64,256]{2,1,0:T(8,128)(2,1)} %param.11) | copy-start | bytes 1572868
  6.5 151.5 %all-gather.2.cloned.1.call-start = ((), (), s32[]{:S(2)}) async-start(), calls=%async_computation | async-start | bytes 2228224 | tf_op jit(solution)/shard_map/all_gather | solution.py:90
  85.1 38.2 %collective-permute-start.3 = (f32[64,64]{1,0:T(8,128)S(1)}, f32[64,64]{1,0:T(8,128)S(1)}, u32[]{:S(2)}, u32[]{:S(2)}) collective-permute-start(f32[64,64]{1,0:T(8,128)S(1)} %psum.7), channel_id=1, source_target_pairs={{48,0},{64,16},{80,32},{96,48},{112,64},{128,80},{144,96},{160,112... | collective-permute-start | bytes 49160 | tf_op jit(solution)/shard_map/ppermute | solution.py:17
  86.4 28.1 %collective-permute-start.2 = (f32[64,64]{1,0:T(8,128)S(1)}, f32[64,64]{1,0:T(8,128)S(1)}, u32[]{:S(2)}, u32[]{:S(2)}) collective-permute-start(f32[64,64]{1,0:T(8,128)S(1)} %psum.7), channel_id=1, source_target_pairs={{32,0},{48,16},{64,32},{80,48},{96,64},{112,80},{128,96},{144,112}... | collective-permute-start | bytes 49160 | tf_op jit(solution)/shard_map/ppermute | solution.py:17
  88.5 28.3 %collective-permute-start.1 = (f32[64,64]{1,0:T(8,128)S(1)}, f32[64,64]{1,0:T(8,128)S(1)}, u32[]{:S(2)}, u32[]{:S(2)}) collective-permute-start(f32[64,64]{1,0:T(8,128)S(1)} %psum.7), channel_id=1, source_target_pairs={{0,32},{16,48},{32,64},{48,80},{64,96},{80,112},{96,128},{112,144}... | collective-permute-start | bytes 49160 | tf_op jit(solution)/shard_map/ppermute | solution.py:17
  92.8 64.0 %collective-permute-start = (f32[64,64]{1,0:T(8,128)S(1)}, f32[64,64]{1,0:T(8,128)S(1)}, u32[]{:S(2)}, u32[]{:S(2)}) collective-permute-start(f32[64,64]{1,0:T(8,128)S(1)} %psum.7), channel_id=1, source_target_pairs={{0,48},{16,64},{32,80},{48,96},{64,112},{80,128},{96,144},{112,160... | collective-permute-start | bytes 49160 | tf_op jit(solution)/shard_map/ppermute | solution.py:17
  98.1 14.2 %collective-permute-start.4 = (f32[64,64]{1,0:T(8,128)S(1)}, f32[64,64]{1,0:T(8,128)S(1)}, u32[]{:S(2)}, u32[]{:S(2)}) collective-permute-start(f32[64,64]{1,0:T(8,128)S(1)} %fusion.31), channel_id=1, source_target_pairs={{0,16},{16,0},{32,48},{48,32},{64,80},{80,64},{96,112},{112,96},{1... | collective-permute-start | bytes 49160 | tf_op jit(solution)/shard_map/ppermute | solution.py:11
  105.1 6.9 %copy-start.6 = (s32[16]{0:T(128)S(1)}, s32[16]{0:T(128)}, u32[]{:S(2)}) copy-start(s32[16]{0:T(128)} %param.16) | copy-start | bytes 196
  105.1 7.0 %copy-start.5 = (s32[16,8]{0,1:T(8,128)S(1)}, s32[16,8]{0,1:T(8,128)}, u32[]{:S(2)}) copy-start(s32[16,8]{0,1:T(8,128)} %param.15) | copy-start | bytes 1540
  105.1 52.7 %copy-start.4 = (f32[1,1,64,64]{3,2,1,0:T(8,128)S(1)}, f32[1,1,64,64]{3,2,1,0:T(8,128)}, u32[]{:S(2)}) copy-start(f32[1,1,64,64]{3,2,1,0:T(8,128)} %param.19) | copy-start | bytes 49156
  112.3 27.0 %collective-permute-start.8 = (f32[64,64]{1,0:T(8,128)S(1)}, f32[64,64]{1,0:T(8,128)S(1)}, u32[]{:S(2)}, u32[]{:S(2)}) collective-permute-start(f32[64,64]{1,0:T(8,128)S(1)} %add.117), channel_id=1, source_target_pairs={{96,0},{112,16},{128,32},{144,48},{160,64},{176,80},{192,96},{208,... | collective-permute-start | bytes 49160 | tf_op jit(solution)/shard_map/ppermute | solution.py:17
  114.5 20.3 %collective-permute-start.7 = (f32[64,64]{1,0:T(8,128)S(1)}, f32[64,64]{1,0:T(8,128)S(1)}, u32[]{:S(2)}, u32[]{:S(2)}) collective-permute-start(f32[64,64]{1,0:T(8,128)S(1)} %add.117), channel_id=1, source_target_pairs={{64,0},{80,16},{96,32},{112,48},{128,64},{144,80},{160,96},{176,11... | collective-permute-start | bytes 49160 | tf_op jit(solution)/shard_map/ppermute | solution.py:17
  116.8 20.3 %collective-permute-start.6 = (f32[64,64]{1,0:T(8,128)S(1)}, f32[64,64]{1,0:T(8,128)S(1)}, u32[]{:S(2)}, u32[]{:S(2)}) collective-permute-start(f32[64,64]{1,0:T(8,128)S(1)} %add.117), channel_id=1, source_target_pairs={{0,64},{16,80},{32,96},{48,112},{64,128},{80,144},{96,160},{112,17... | collective-permute-start | bytes 49160 | tf_op jit(solution)/shard_map/ppermute | solution.py:17
  123.3 4.0 %collective-permute-start.9 = (f32[64,64]{1,0:T(8,128)S(1)}, f32[64,64]{1,0:T(8,128)S(1)}, u32[]{:S(2)}, u32[]{:S(2)}) collective-permute-start(f32[64,64]{1,0:T(8,128)S(1)} %fusion.27), channel_id=1, source_target_pairs={{0,32},{16,48},{32,0},{48,16},{64,96},{80,112},{96,64},{112,80},{1... | collective-permute-start | bytes 49160 | tf_op jit(solution)/shard_map/ppermute | solution.py:11
  127.3 27.6 %collective-permute-start.5 = (f32[64,64]{1,0:T(8,128)S(1)}, f32[64,64]{1,0:T(8,128)S(1)}, u32[]{:S(2)}, u32[]{:S(2)}) collective-permute-start(f32[64,64]{1,0:T(8,128)S(1)} %add.117), channel_id=1, source_target_pairs={{0,96},{16,112},{32,128},{48,144},{64,160},{80,176},{96,192},{112,... | collective-permute-start | bytes 49160 | tf_op jit(solution)/shard_map/ppermute | solution.py:17
  134.8 17.2 %collective-permute-start.13 = (f32[64,64]{1,0:T(8,128)S(1)}, f32[64,64]{1,0:T(8,128)S(1)}, u32[]{:S(2)}, u32[]{:S(2)}) collective-permute-start(f32[64,64]{1,0:T(8,128)S(1)} %add.125), channel_id=1, source_target_pairs={{192,0},{208,16},{224,32},{240,48},{193,1},{209,17},{225,33},{241,... | collective-permute-start | bytes 49160 | tf_op jit(solution)/shard_map/ppermute | solution.py:17
  137.1 11.7 %collective-permute-start.12 = (f32[64,64]{1,0:T(8,128)S(1)}, f32[64,64]{1,0:T(8,128)S(1)}, u32[]{:S(2)}, u32[]{:S(2)}) collective-permute-start(f32[64,64]{1,0:T(8,128)S(1)} %add.125), channel_id=1, source_target_pairs={{128,0},{144,16},{160,32},{176,48},{192,64},{208,80},{224,96},{240... | collective-permute-start | bytes 49160 | tf_op jit(solution)/shard_map/ppermute | solution.py:17
  139.3 11.7 %collective-permute-start.11 = (f32[64,64]{1,0:T(8,128)S(1)}, f32[64,64]{1,0:T(8,128)S(1)}, u32[]{:S(2)}, u32[]{:S(2)}) collective-permute-start(f32[64,64]{1,0:T(8,128)S(1)} %add.125), channel_id=1, source_target_pairs={{0,128},{16,144},{32,160},{48,176},{64,192},{80,208},{96,224},{112... | collective-permute-start | bytes 49160 | tf_op jit(solution)/shard_map/ppermute | solution.py:17
  148.8 4.2 %collective-permute-start.10 = (f32[64,64]{1,0:T(8,128)S(1)}, f32[64,64]{1,0:T(8,128)S(1)}, u32[]{:S(2)}, u32[]{:S(2)}) collective-permute-start(f32[64,64]{1,0:T(8,128)S(1)} %add.125), channel_id=1, source_target_pairs={{0,192},{16,208},{32,224},{48,240},{1,193},{17,209},{33,225},{49,2... | collective-permute-start | bytes 49160 | tf_op jit(solution)/shard_map/ppermute | solution.py:17
  165.3 2.4 %copy-start.2 = (f32[16,64,64]{2,1,0:T(8,128)S(1)}, f32[16,64,64]{2,1,0:T(8,128)}, u32[]{:S(2)}) copy-start(f32[16,64,64]{2,1,0:T(8,128)} %param.18) | copy-start | bytes 786436
  165.3 4.0 %copy-start.3 = (bf16[16,64,256]{2,1,0:T(8,128)(2,1)S(1)}, bf16[16,64,256]{2,1,0:T(8,128)(2,1)}, u32[]{:S(2)}) copy-start(bf16[16,64,256]{2,1,0:T(8,128)(2,1)} %param.12) | copy-start | bytes 1572868
Sparse Core Ops, SparseCore 0:
  97.3 47.2 all-gather.1
where the time goes:
time: 179 us; the launch traced here: 177 us
  blocking collectives  74.6 us (42%)
  starting transfers between devices  42.7 us (24%)
  matrix products  34.2 us (19%)
  between operations  13.8 us (8%)
  local copies, waits for them, and re-layouts  8.41 us (5%)
  waiting for transfers between devices  2.66 us (1%)
    psum x1, blocking collectives, on_device(): group_node = lax.psum(device_term, 'list')  74.6 us
    ppermute x12, starting transfers between devices, shifted(): return lax.ppermute(array, axis, pairs)  38.9 us
    dot_general x12, matrix products, upper_exchange(): contribution = jnp.dot(source, matrices[slot_index].T, precision=highest)  11.4 us
    dot_general x1, matrix products, on_device(): jnp.einsum('ckrm,cknm->crn', neighbours, near_blocks, preferred_element_t...  6.84 us
    reshape x1, local copies, waits for them, and re-layouts, on_device(): selected.reshape(leaf_local, far_slots, skeleton.shape[1], skeleton.shape...  4.26 us
    ppermute x2, starting transfers between devices, partner(): lax.ppermute(array, axis, [(i, i ^ 1 << distance) for i in range(lax.axis...  3.79 us
  transfers between devices with their start and end apart: 15, of which 1 were waited for; matrix products, arithmetic and copies ran while one was open for 15% of the time, Pallas kernels for 0%

commit v1 on v0

--- a/solution.py
+++ b/solution.py
@@ -79,7 +79,7 @@
         "irb,iba->ra", skeleton.astype(jnp.float32), leaf_transfer, precision=highest
     )
     device_term = jnp.dot(device_node, device_transfer[0, 0], precision=highest)
-    group_node = lax.psum(device_term, "list")
+    group_node = jnp.sum(lax.all_gather(device_term, "list"), axis=0)
     top_down = upper_exchange(group_node, tree_transfer, level_coupling)
     device_down = jnp.dot(top_down, device_transfer[0, 0].T, precision=highest)
     from_above = jnp.einsum("rd,ild->irl", device_down, leaf_transfer, precision=highest)

time: 179 us -> 130 us (0.73)
  blocking collectives: 74.6 us -> 26.2 us
    psum x1 -> x0, blocking collectives: 74.6 us -> none  [on_device(): group_node = lax.psum(device_term, 'list')]
    all_gather x0 -> x1, blocking collectives: none -> 26.2 us  [on_device(): group_node = jnp.sum(lax.all_gather(device_term, 'list'), axis=0)]
  transfers between devices with their start and end apart: 15 -> 15, of which waited for: 1 -> 1; matrix products, arithmetic and copies ran while one was open for 15% -> 20% of each run, Pallas kernels for 0% -> 0%
where the time goes in v1:
time: 130 us; the launch traced here: 129 us
  starting transfers between devices  42.7 us (33%)
  matrix products  34.1 us (26%)
  blocking collectives  26.2 us (20%)
  between operations  13.8 us (11%)
  local copies, waits for them, and re-layouts  7.73 us (6%)
  waiting for transfers between devices  2.66 us (2%)
    ppermute x12, starting transfers between devices, shifted(): return lax.ppermute(array, axis, pairs)  38.9 us
    all_gather x1, blocking collectives, on_device(): group_node = jnp.sum(lax.all_gather(device_term, 'list'), axis=0)  26.2 us
    dot_general x12, matrix products, upper_exchange(): contribution = jnp.dot(source, matrices[slot_index].T, precision=highest)  11.4 us
    dot_general x1, matrix products, on_device(): jnp.einsum('ckrm,cknm->crn', neighbours, near_blocks, preferred_element_t...  6.69 us
    reshape x1, local copies, waits for them, and re-layouts, on_device(): selected.reshape(leaf_local, far_slots, skeleton.shape[1], skeleton.shape...  4.25 us
    ppermute x2, starting transfers between devices, partner(): lax.ppermute(array, axis, [(i, i ^ 1 << distance) for i in range(lax.axis...  3.79 us
    dot_general x1, matrix products, on_device(): collected = jnp.dot(hits, piece, preferred_element_type=jnp.float32)  3.06 us
  transfers between devices with their start and end apart: 15, of which 1 were waited for; matrix products, arithmetic and copies ran while one was open for 20% of the time, Pallas kernels for 0%

profile of v1, /device:TPU:32, one launch (start us, length us, event | category | flops | bytes accessed | tf_op | source)
XLA Modules:
  0.0 128.5 jit_solution(16155438489979381765)
XLA Ops:
  6.5 1.6 %convolution_convert_fusion.1 = bf16[16,64,64]{2,1,0:T(8,128)(2,1)S(1)} fusion(bf16[16,64,256]{2,1,0:T(8,128)(2,1)} %param.11, bf16[16,64,256]{2,1,0:T(8,128)(2,1)} %param.12), kind=kOutput, calls=%fused_computation.12 | convolution fusion | flops 33619968 | bytes 1179648 | tf_op jit(solution)/shard_map/crm,ckm->crk/dot_general | solution.py:75
  8.2 1.4 %convolution_bitcast_fusion.3 = f32[64,64]{1,0:T(8,128)S(1)} fusion(bf16[16,64,64]{2,1,0:T(8,128)(2,1)S(1)} %convolution_convert_fusion.1, f32[16,64,64]{2,1,0:T(8,128)} %param.18), kind=kOutput, calls=%fused_computation.37 | convolution fusion | flops 50331648 | bytes 409600 | tf_op jit(solution)/shard_map/irb,iba->ra/dot_general | solution.py:78
  10.5 26.2 %all-gather = f32[1024,64]{1,0:T(8,128)} all-gather(f32[64,64]{1,0:T(8,128)S(1)} %fusion.34), channel_id=2, replica_groups=mesh['leaf'=16,'list'=16] {'list'}, dimensions={0}, use_global_device_ids=true | all-gather | bytes 278528 | tf_op jit(solution)/shard_map/all_gather | solution.py:82
  36.8 1.1 reduce_sum.9
  37.9 1.3 %collective-permute-start.3 = (f32[64,64]{1,0:T(8,128)S(1)}, f32[64,64]{1,0:T(8,128)S(1)}, u32[]{:S(2)}, u32[]{:S(2)}) collective-permute-start(f32[64,64]{1,0:T(8,128)S(1)} %reduce_sum.9), channel_id=1, source_target_pairs={{48,0},{64,16},{80,32},{96,48},{112,64},{128,80},{144,96},{160,112... | collective-permute-start | bytes 49160 | tf_op jit(solution)/shard_map/ppermute | solution.py:17
  39.2 2.0 %collective-permute-start.2 = (f32[64,64]{1,0:T(8,128)S(1)}, f32[64,64]{1,0:T(8,128)S(1)}, u32[]{:S(2)}, u32[]{:S(2)}) collective-permute-start(f32[64,64]{1,0:T(8,128)S(1)} %reduce_sum.9), channel_id=1, source_target_pairs={{32,0},{48,16},{64,32},{80,48},{96,64},{112,80},{128,96},{144,112}... | collective-permute-start | bytes 49160 | tf_op jit(solution)/shard_map/ppermute | solution.py:17
  41.2 4.4 %collective-permute-start.1 = (f32[64,64]{1,0:T(8,128)S(1)}, f32[64,64]{1,0:T(8,128)S(1)}, u32[]{:S(2)}, u32[]{:S(2)}) collective-permute-start(f32[64,64]{1,0:T(8,128)S(1)} %reduce_sum.9), channel_id=1, source_target_pairs={{0,32},{16,48},{32,64},{48,80},{64,96},{80,112},{96,128},{112,144}... | collective-permute-start | bytes 49160 | tf_op jit(solution)/shard_map/ppermute | solution.py:17
  45.6 3.4 %collective-permute-start = (f32[64,64]{1,0:T(8,128)S(1)}, f32[64,64]{1,0:T(8,128)S(1)}, u32[]{:S(2)}, u32[]{:S(2)}) collective-permute-start(f32[64,64]{1,0:T(8,128)S(1)} %reduce_sum.9), channel_id=1, source_target_pairs={{0,48},{16,64},{32,80},{48,96},{64,112},{80,128},{96,144},{112,160... | collective-permute-start | bytes 49160 | tf_op jit(solution)/shard_map/ppermute | solution.py:17
  50.8 3.3 %collective-permute-start.4 = (f32[64,64]{1,0:T(8,128)S(1)}, f32[64,64]{1,0:T(8,128)S(1)}, u32[]{:S(2)}, u32[]{:S(2)}) collective-permute-start(f32[64,64]{1,0:T(8,128)S(1)} %fusion.31), channel_id=1, source_target_pairs={{0,16},{16,0},{32,48},{48,32},{64,80},{80,64},{96,112},{112,96},{1... | collective-permute-start | bytes 49160 | tf_op jit(solution)/shard_map/ppermute | solution.py:11
  54.5 2.0 %gather_fusion = bf16[64,64,256]{2,1,0:T(8,128)(2,1)} fusion(bf16[16,64,256]{2,1,0:T(8,128)(2,1)S(1)} %copy-done.1, s32[1024]{0:T(1024)S(1)} %pad_clamp_fusion), kind=kCustom, calls=%fused_computation | custom fusion | bytes 4194560 | tf_op jit(solution)/shard_map/jit(_take)/gather | solution.py:103
  56.5 6.7 %fusion.3 = f32[16,64,256]{2,1,0:T(8,128)S(1)} fusion(bf16[16,4,256,256]{3,2,1,0:T(8,128)(2,1)} %param.13, bf16[16,4,64,256]{3,2,1,0:T(8,128)(2,1)} %bitcast.101, pred[16,4]{1,0:T(8,128)(4,1)S(1)} %copy.16), kind=kOutput, calls=%fused_computation.5 | convolution fusion | flops 537919488 | bytes 11534400 | tf_op jit(solution)/shard_map/ckrm,cknm->crn/dot_general | solution.py:107
  63.5 1.3 %collective-permute-start.8 = (f32[64,64]{1,0:T(8,128)S(1)}, f32[64,64]{1,0:T(8,128)S(1)}, u32[]{:S(2)}, u32[]{:S(2)}) collective-permute-start(f32[64,64]{1,0:T(8,128)S(1)} %add.115), channel_id=1, source_target_pairs={{96,0},{112,16},{128,32},{144,48},{160,64},{176,80},{192,96},{208,... | collective-permute-start | bytes 49160 | tf_op jit(solution)/shard_map/ppermute | solution.py:17
  65.8 1.3 %collective-permute-start.7 = (f32[64,64]{1,0:T(8,128)S(1)}, f32[64,64]{1,0:T(8,128)S(1)}, u32[]{:S(2)}, u32[]{:S(2)}) collective-permute-start(f32[64,64]{1,0:T(8,128)S(1)} %add.115), channel_id=1, source_target_pairs={{64,0},{80,16},{96,32},{112,48},{128,64},{144,80},{160,96},{176,11... | collective-permute-start | bytes 49160 | tf_op jit(solution)/shard_map/ppermute | solution.py:17
  68.0 5.5 %collective-permute-start.6 = (f32[64,64]{1,0:T(8,128)S(1)}, f32[64,64]{1,0:T(8,128)S(1)}, u32[]{:S(2)}, u32[]{:S(2)}) collective-permute-start(f32[64,64]{1,0:T(8,128)S(1)} %add.115), channel_id=1, source_target_pairs={{0,64},{16,80},{32,96},{48,112},{64,128},{80,144},{96,160},{112,17... | collective-permute-start | bytes 49160 | tf_op jit(solution)/shard_map/ppermute | solution.py:17
  76.0 2.6 %collective-permute-done.9 = f32[64,64]{1,0:T(8,128)S(1)} collective-permute-done((f32[64,64]{1,0:T(8,128)S(1)}, f32[64,64]{1,0:T(8,128)S(1)}, u32[]{:S(2)}, u32[]{:S(2)}) %collective-permute-start.9) | collective-permute-done | bytes 16416 | tf_op jit(solution)/shard_map/ppermute | solution.py:11
  78.6 7.5 %collective-permute-start.5 = (f32[64,64]{1,0:T(8,128)S(1)}, f32[64,64]{1,0:T(8,128)S(1)}, u32[]{:S(2)}, u32[]{:S(2)}) collective-permute-start(f32[64,64]{1,0:T(8,128)S(1)} %add.115), channel_id=1, source_target_pairs={{0,96},{16,112},{32,128},{48,144},{64,160},{80,176},{96,192},{112,... | collective-permute-start | bytes 49160 | tf_op jit(solution)/shard_map/ppermute | solution.py:17
  86.0 1.3 %collective-permute-start.13 = (f32[64,64]{1,0:T(8,128)S(1)}, f32[64,64]{1,0:T(8,128)S(1)}, u32[]{:S(2)}, u32[]{:S(2)}) collective-permute-start(f32[64,64]{1,0:T(8,128)S(1)} %add.123), channel_id=1, source_target_pairs={{192,0},{208,16},{224,32},{240,48},{193,1},{209,17},{225,33},{241,... | collective-permute-start | bytes 49160 | tf_op jit(solution)/shard_map/ppermute | solution.py:17
  88.3 1.3 %collective-permute-start.12 = (f32[64,64]{1,0:T(8,128)S(1)}, f32[64,64]{1,0:T(8,128)S(1)}, u32[]{:S(2)}, u32[]{:S(2)}) collective-permute-start(f32[64,64]{1,0:T(8,128)S(1)} %add.123), channel_id=1, source_target_pairs={{128,0},{144,16},{160,32},{176,48},{192,64},{208,80},{224,96},{240... | collective-permute-start | bytes 49160 | tf_op jit(solution)/shard_map/ppermute | solution.py:17
  90.6 8.5 %collective-permute-start.11 = (f32[64,64]{1,0:T(8,128)S(1)}, f32[64,64]{1,0:T(8,128)S(1)}, u32[]{:S(2)}, u32[]{:S(2)}) collective-permute-start(f32[64,64]{1,0:T(8,128)S(1)} %add.123), channel_id=1, source_target_pairs={{0,128},{16,144},{32,160},{48,176},{64,192},{80,208},{96,224},{112... | collective-permute-start | bytes 49160 | tf_op jit(solution)/shard_map/ppermute | solution.py:17
  100.0 1.3 %collective-permute-start.10 = (f32[64,64]{1,0:T(8,128)S(1)}, f32[64,64]{1,0:T(8,128)S(1)}, u32[]{:S(2)}, u32[]{:S(2)}) collective-permute-start(f32[64,64]{1,0:T(8,128)S(1)} %add.123), channel_id=1, source_target_pairs={{0,192},{16,208},{32,224},{48,240},{1,193},{17,209},{33,225},{49,2... | collective-permute-start | bytes 49160 | tf_op jit(solution)/shard_map/ppermute | solution.py:17
  109.3 3.1 %convolution_convert_fusion = bf16[128,4096]{1,0:T(8,128)(2,1)} fusion(bf16[256,4096]{1,0:T(8,128)(2,1)} %all-gather.3.cloned.1.call-done, s32[128]{0:T(128)S(1)} %eq.37, pred[128]{0:T(512)(128)(4,1)S(1)} %lt.70), kind=kOutput, calls=%fused_computation.1 | convolution fusion | flops 269025280 | bytes 3146368 | tf_op jit(solution)/shard_map/dot_general | solution.py:93
  112.3 4.3 %reshape.87 = bf16[16,8,64,64]{3,2,1,0:T(8,128)(2,1)} reshape(bf16[128,4096]{1,0:T(8,128)(2,1)} %convolution_convert_fusion) | data formatting | bytes 2097152 | tf_op jit(solution)/shard_map/reshape | solution.py:95
  116.6 2.4 %convolution_bitcast_fusion = f32[16,64,64]{2,1,0:T(8,128)S(1)} fusion(bf16[16,8,64,64]{3,2,1,0:T(8,128)(2,1)} %reshape.87, bf16[16,8,64,64]{3,2,1,0:T(8,128)(2,1)S(1)} %copy-done), kind=kOutput, calls=%fused_computation.8 | convolution fusion | flops 67108864 | bytes 2359296 | tf_op jit(solution)/shard_map/ckrb,ckab->cra/dot_general | solution.py:96
  119.0 1.6 %fusion.8 = bf16[16,64,64]{2,1,0:T(8,128)(2,1)S(1)} fusion(f32[16,64,64]{2,1,0:T(8,128)S(1)} %convolution_bitcast_fusion, f32[64,64,1]{1,0,2:T(8,128)S(1)} %convolution_bitcast_fusion.2, f32[16,64,64]{2,1,0:T(8,128)S(1)} %copy-done.2), kind=kOutput, calls=%fused_computation.11 | convolution fusion | flops 50462720 | bytes 671744 | tf_op jit(solution)/shard_map/rd,ild->irl/dot_general | solution.py:85
  (65 shorter events, 19.5 us)
Async XLA Ops:
  6.5 110.1 %copy-start = (bf16[16,8,64,64]{3,2,1,0:T(8,128)(2,1)S(1)}, bf16[16,8,64,64]{3,2,1,0:T(8,128)(2,1)}, u32[]{:S(2)}) copy-start(bf16[16,8,64,64]{3,2,1,0:T(8,128)(2,1)} %param.17) | copy-start | bytes 3145732
  6.5 47.9 %copy-start.1 = (bf16[16,64,256]{2,1,0:T(8,128)(2,1)S(1)}, bf16[16,64,256]{2,1,0:T(8,128)(2,1)}, u32[]{:S(2)}) copy-start(bf16[16,64,256]{2,1,0:T(8,128)(2,1)} %param.11) | copy-start | bytes 1572868
  6.5 47.6 %copy-start.5 = (s32[16,4]{0,1:T(4,128)S(1)}, s32[16,4]{0,1:T(4,128)}, u32[]{:S(2)}) copy-start(s32[16,4]{0,1:T(4,128)} %param.14) | copy-start | bytes 772
  6.5 102.7 %all-gather.3.cloned.1.call-start = ((), (), s32[]{:S(2)}) async-start(), calls=%async_computation | async-start | bytes 2228224 | tf_op jit(solution)/shard_map/all_gather | solution.py:90
  37.9 36.7 %collective-permute-start.3 = (f32[64,64]{1,0:T(8,128)S(1)}, f32[64,64]{1,0:T(8,128)S(1)}, u32[]{:S(2)}, u32[]{:S(2)}) collective-permute-start(f32[64,64]{1,0:T(8,128)S(1)} %reduce_sum.9), channel_id=1, source_target_pairs={{48,0},{64,16},{80,32},{96,48},{112,64},{128,80},{144,96},{160,112... | collective-permute-start | bytes 49160 | tf_op jit(solution)/shard_map/ppermute | solution.py:17
  39.2 26.6 %collective-permute-start.2 = (f32[64,64]{1,0:T(8,128)S(1)}, f32[64,64]{1,0:T(8,128)S(1)}, u32[]{:S(2)}, u32[]{:S(2)}) collective-permute-start(f32[64,64]{1,0:T(8,128)S(1)} %reduce_sum.9), channel_id=1, source_target_pairs={{32,0},{48,16},{64,32},{80,48},{96,64},{112,80},{128,96},{144,112}... | collective-permute-start | bytes 49160 | tf_op jit(solution)/shard_map/ppermute | solution.py:17
  41.2 26.8 %collective-permute-start.1 = (f32[64,64]{1,0:T(8,128)S(1)}, f32[64,64]{1,0:T(8,128)S(1)}, u32[]{:S(2)}, u32[]{:S(2)}) collective-permute-start(f32[64,64]{1,0:T(8,128)S(1)} %reduce_sum.9), channel_id=1, source_target_pairs={{0,32},{16,48},{32,64},{48,80},{64,96},{80,112},{96,128},{112,144}... | collective-permute-start | bytes 49160 | tf_op jit(solution)/shard_map/ppermute | solution.py:17
  45.6 62.5 %collective-permute-start = (f32[64,64]{1,0:T(8,128)S(1)}, f32[64,64]{1,0:T(8,128)S(1)}, u32[]{:S(2)}, u32[]{:S(2)}) collective-permute-start(f32[64,64]{1,0:T(8,128)S(1)} %reduce_sum.9), channel_id=1, source_target_pairs={{0,48},{16,64},{32,80},{48,96},{64,112},{80,128},{96,144},{112,160... | collective-permute-start | bytes 49160 | tf_op jit(solution)/shard_map/ppermute | solution.py:17
  50.8 12.7 %collective-permute-start.4 = (f32[64,64]{1,0:T(8,128)S(1)}, f32[64,64]{1,0:T(8,128)S(1)}, u32[]{:S(2)}, u32[]{:S(2)}) collective-permute-start(f32[64,64]{1,0:T(8,128)S(1)} %fusion.31), channel_id=1, source_target_pairs={{0,16},{16,0},{32,48},{48,32},{64,80},{80,64},{96,112},{112,96},{1... | collective-permute-start | bytes 49160 | tf_op jit(solution)/shard_map/ppermute | solution.py:11
  56.5 6.7 %copy-start.7 = (s32[16]{0:T(128)S(1)}, s32[16]{0:T(128)}, u32[]{:S(2)}) copy-start(s32[16]{0:T(128)} %param.16) | copy-start | bytes 196
  56.5 6.9 %copy-start.6 = (s32[16,8]{0,1:T(8,128)S(1)}, s32[16,8]{0,1:T(8,128)}, u32[]{:S(2)}) copy-start(s32[16,8]{0,1:T(8,128)} %param.15) | copy-start | bytes 1540
  56.5 52.6 %copy-start.4 = (f32[1,1,64,64]{3,2,1,0:T(8,128)S(1)}, f32[1,1,64,64]{3,2,1,0:T(8,128)}, u32[]{:S(2)}) copy-start(f32[1,1,64,64]{3,2,1,0:T(8,128)} %param.19) | copy-start | bytes 49156
  63.5 27.0 %collective-permute-start.8 = (f32[64,64]{1,0:T(8,128)S(1)}, f32[64,64]{1,0:T(8,128)S(1)}, u32[]{:S(2)}, u32[]{:S(2)}) collective-permute-start(f32[64,64]{1,0:T(8,128)S(1)} %add.115), channel_id=1, source_target_pairs={{96,0},{112,16},{128,32},{144,48},{160,64},{176,80},{192,96},{208,... | collective-permute-start | bytes 49160 | tf_op jit(solution)/shard_map/ppermute | solution.py:17
  65.8 20.3 %collective-permute-start.7 = (f32[64,64]{1,0:T(8,128)S(1)}, f32[64,64]{1,0:T(8,128)S(1)}, u32[]{:S(2)}, u32[]{:S(2)}) collective-permute-start(f32[64,64]{1,0:T(8,128)S(1)} %add.115), channel_id=1, source_target_pairs={{64,0},{80,16},{96,32},{112,48},{128,64},{144,80},{160,96},{176,11... | collective-permute-start | bytes 49160 | tf_op jit(solution)/shard_map/ppermute | solution.py:17
  68.0 20.3 %collective-permute-start.6 = (f32[64,64]{1,0:T(8,128)S(1)}, f32[64,64]{1,0:T(8,128)S(1)}, u32[]{:S(2)}, u32[]{:S(2)}) collective-permute-start(f32[64,64]{1,0:T(8,128)S(1)} %add.115), channel_id=1, source_target_pairs={{0,64},{16,80},{32,96},{48,112},{64,128},{80,144},{96,160},{112,17... | collective-permute-start | bytes 49160 | tf_op jit(solution)/shard_map/ppermute | solution.py:17
  74.6 4.0 %collective-permute-start.9 = (f32[64,64]{1,0:T(8,128)S(1)}, f32[64,64]{1,0:T(8,128)S(1)}, u32[]{:S(2)}, u32[]{:S(2)}) collective-permute-start(f32[64,64]{1,0:T(8,128)S(1)} %fusion.27), channel_id=1, source_target_pairs={{0,32},{16,48},{32,0},{48,16},{64,96},{80,112},{96,64},{112,80},{1... | collective-permute-start | bytes 49160 | tf_op jit(solution)/shard_map/ppermute | solution.py:11
  78.6 27.6 %collective-permute-start.5 = (f32[64,64]{1,0:T(8,128)S(1)}, f32[64,64]{1,0:T(8,128)S(1)}, u32[]{:S(2)}, u32[]{:S(2)}) collective-permute-start(f32[64,64]{1,0:T(8,128)S(1)} %add.115), channel_id=1, source_target_pairs={{0,96},{16,112},{32,128},{48,144},{64,160},{80,176},{96,192},{112,... | collective-permute-start | bytes 49160 | tf_op jit(solution)/shard_map/ppermute | solution.py:17
  86.0 17.2 %collective-permute-start.13 = (f32[64,64]{1,0:T(8,128)S(1)}, f32[64,64]{1,0:T(8,128)S(1)}, u32[]{:S(2)}, u32[]{:S(2)}) collective-permute-start(f32[64,64]{1,0:T(8,128)S(1)} %add.123), channel_id=1, source_target_pairs={{192,0},{208,16},{224,32},{240,48},{193,1},{209,17},{225,33},{241,... | collective-permute-start | bytes 49160 | tf_op jit(solution)/shard_map/ppermute | solution.py:17
  88.3 11.7 %collective-permute-start.12 = (f32[64,64]{1,0:T(8,128)S(1)}, f32[64,64]{1,0:T(8,128)S(1)}, u32[]{:S(2)}, u32[]{:S(2)}) collective-permute-start(f32[64,64]{1,0:T(8,128)S(1)} %add.123), channel_id=1, source_target_pairs={{128,0},{144,16},{160,32},{176,48},{192,64},{208,80},{224,96},{240... | collective-permute-start | bytes 49160 | tf_op jit(solution)/shard_map/ppermute | solution.py:17
  90.6 11.7 %collective-permute-start.11 = (f32[64,64]{1,0:T(8,128)S(1)}, f32[64,64]{1,0:T(8,128)S(1)}, u32[]{:S(2)}, u32[]{:S(2)}) collective-permute-start(f32[64,64]{1,0:T(8,128)S(1)} %add.123), channel_id=1, source_target_pairs={{0,128},{16,144},{32,160},{48,176},{64,192},{80,208},{96,224},{112... | collective-permute-start | bytes 49160 | tf_op jit(solution)/shard_map/ppermute | solution.py:17
  100.0 4.2 %collective-permute-start.10 = (f32[64,64]{1,0:T(8,128)S(1)}, f32[64,64]{1,0:T(8,128)S(1)}, u32[]{:S(2)}, u32[]{:S(2)}) collective-permute-start(f32[64,64]{1,0:T(8,128)S(1)} %add.123), channel_id=1, source_target_pairs={{0,192},{16,208},{32,224},{48,240},{1,193},{17,209},{33,225},{49,2... | collective-permute-start | bytes 49160 | tf_op jit(solution)/shard_map/ppermute | solution.py:17
  116.6 2.4 %copy-start.2 = (f32[16,64,64]{2,1,0:T(8,128)S(1)}, f32[16,64,64]{2,1,0:T(8,128)}, u32[]{:S(2)}) copy-start(f32[16,64,64]{2,1,0:T(8,128)} %param.18) | copy-start | bytes 786436
  116.6 4.0 %copy-start.3 = (bf16[16,64,256]{2,1,0:T(8,128)(2,1)S(1)}, bf16[16,64,256]{2,1,0:T(8,128)(2,1)}, u32[]{:S(2)}) copy-start(bf16[16,64,256]{2,1,0:T(8,128)(2,1)} %param.12) | copy-start | bytes 1572868
Sparse Core Ops, SparseCore 0:
  50.0 50.2 all-gather.2
